TPU v7x, 128 devices: a whole 4x4x4 slice. The times are simulated.
128 devices in a mesh: row: 8 (over z_hi, y), col: 16 (over z_lo, x, core).
Axes of the slice: x: 4, y: 4, z: 4 (z_hi: 2, z_lo: 2; z = z_hi * 2 + z_lo), core: 2. Of those that a mesh axis runs over, the one named last changes fastest.
Arguments:
- features: float32 [2, 131072, 256], P(None, ('row', 'col')), may hold values from -7 to 7
- adj_vals: bfloat16 [2, 1024, 20, 128, 128], P(None, ('row', 'col')), may hold values from 0.049804688 to 1
- blk_cols: int32 [2, 1024, 20], P(None, ('row', 'col')), may hold values from 0 to 11
- blk_count: int32 [2, 1024], P(None, ('row', 'col')), may hold values from 1 to 20
- send_list: int32 [2, 128, 512], P(None, ('row', 'col')), may hold values from 0 to 1023
- weight: float32 [256, 256], replicated, may hold values from -0.375 to 0.375
- cand_tiles: int32 [8, 16, 2, 48], P('row', 'col'), may hold values from 0 to 127, as said below
- cand_count: int32 [8, 16], P('row', 'col'), may hold values from 8 to 48, as said below
Outputs:
- log_plan: float32 [8, 16, 48, 128, 128], P('row', 'col')
- row_potential: float32 [8, 16, 1024], P('row')
- col_potential: float32 [8, 16, 1024], P(None, 'col')
Inputs may be any that keep to these rules, and one draw needn't show every extreme that they name: Blocks at or past blk_count are padding. send_list[g, q, p * 4 + i] is the i-th own row that partition q sends to partition p. `cand_tiles`: every slot, live or not, holds a valid pair; no live pair repeats on one device; every tile of every source group and of every target group lies in some live slot; for each device and each partition of its row, at most 3 of the device's 48 slots name source tiles of that partition, and on every device some partition has exactly 3. `cand_count`: some device has all 48 slots live.
All inputs are finite; a program needn't handle non-finite values.
Results may differ from a plain program's by a relative error of at most 0.0003.
Values sent between devices are 32-bit elements; how exact they have to be, the bound alone decides.
A program may use at most 128 MiB of HBM per device.

v0:
```python
import math
import jax
import jax.numpy as jnp
from jax import lax
from jax.sharding import Mesh
from jax.sharding import PartitionSpec as P

TILE = 128
TD = 8
CAP = 48
ITERS = 2
COL = ("col_0", "col_1", "col_2")
ROW_COL = ("row", "col_0", "col_1", "col_2")
HIGHEST = lax.Precision.HIGHEST
SHARPNESS = 2.0
NEGATIVE = -1e30


def joined_all(array, axes, combine):
    for axis in axes:
        pieces = jax.tree.map(lambda part: lax.all_gather(part, axis), array)
        array = jax.tree.map(lambda part: part[0], pieces)
        for k in range(1, lax.axis_size(axis)):
            array = combine(array, jax.tree.map(lambda part: part[k], pieces))
    return array


def from_everyone(array, axis):
    size = lax.axis_size(axis)
    return lax.all_to_all(
        jnp.broadcast_to(array[None], (size, *array.shape)), axis, 0, 0, tiled=True
    )


def gathered_once(array, axis):
    leaves = jax.tree.leaves(array)
    turns = sorted(range(len(leaves)), key=lambda k: -leaves[k].size)
    width = (1, *leaves[turns[0]].shape)[-1]
    lines = [
        jnp.pad(leaves[k].reshape(-1), (0, -leaves[k].size % width)).reshape(-1, width)
        for k in turns
    ]
    both, at, found = (from_everyone(jnp.concatenate(lines), axis), 0, {})
    for k, line in zip(turns, lines):
        share = both[:, at : at + len(line)].reshape(len(both), -1)
        found[k] = share[:, : leaves[k].size].reshape(-1, *leaves[k].shape)
        at += len(line)
    numbers = iter(range(len(leaves)))
    return jax.tree.map(lambda _: found[next(numbers)], array)


def gathered_by_type(array, axis):
    leaves, found = (jax.tree.leaves(array), {})
    for leading, a in enumerate(leaves):
        if leading not in found:
            alike = [k for k, b in enumerate(leaves) if b.dtype == a.dtype]
            got = (
                gathered_once([leaves[k] for k in alike], axis)
                if len(alike) > 1
                else [from_everyone(a, axis)]
            )
            for k, b in zip(alike, got):
                found[k] = b
    numbers = iter(range(len(leaves)))
    return jax.tree.map(lambda _: found[next(numbers)], array)


def joined_by_halves(pieces, combine):
    while len(jax.tree.leaves(pieces)[0]) > 1:
        pieces = jax.vmap(combine)(
            *(jax.tree.map(lambda part: part[side::2], pieces) for side in (0, 1))
        )
    return jax.tree.map(lambda part: part[0], pieces)


def combined_all(array, axis, combine):
    pieces = gathered_by_type(array, axis)
    return joined_by_halves(pieces, combine)


def aggregate(lookup, block_vals, block_cols, block_count, weight, own_rows):
    num_tiles = block_vals.shape[0]
    listed = (jnp.arange(block_vals.shape[1])[None, :] < block_count[:, None]).astype(jnp.float32)

    def add_block(state_pair, block_index):
        summed, degree = state_pair
        weights_now = (
            block_vals[:, block_index].astype(jnp.float32) * listed[:, block_index][:, None, None]
        )
        picked = lookup[block_cols[:, block_index]]
        summed = summed + jnp.einsum("tij,tjd->tid", weights_now, picked, precision=HIGHEST)
        degree = degree + jnp.sum(weights_now, axis=2)
        return ((summed, degree), None)

    start_sum = jnp.zeros((num_tiles, TILE, lookup.shape[2]), jnp.float32)
    start_deg = jnp.zeros((num_tiles, TILE), jnp.float32)
    (summed, degree), unused = lax.scan(
        add_block, (start_sum, start_deg), jnp.arange(block_vals.shape[1])
    )
    mixed_rows = (summed / jnp.sqrt(degree)[:, :, None]).reshape(num_tiles * TILE, -1)
    return own_rows + jax.nn.relu(jnp.dot(mixed_rows, weight, precision=HIGHEST))


def pick_rows(source_rows, picked_rows):
    return source_rows[picked_rows]


def combine_lse(first_pair, second_pair):
    larger = jnp.maximum(first_pair[0], second_pair[0])
    merged_sum = first_pair[1] * jnp.exp(first_pair[0] - larger) + second_pair[1] * jnp.exp(
        second_pair[0] - larger
    )
    return (larger, merged_sum)


def lookup_rows(one_hot, table_values):
    return jnp.dot(one_hot, table_values, precision=HIGHEST)


def row_potential_of(values, grouped, picker, live_float):
    slot_max = jnp.max(values, axis=2)
    group_max = jnp.max(jnp.where(grouped[:, :, None], slot_max[:, None, :], NEGATIVE), axis=0)
    shift_back = lookup_rows(picker, group_max)
    slot_sums = jnp.sum(jnp.exp(values - shift_back[:, :, None]), axis=2)
    group_sum = jnp.einsum("sr,sc->rc", live_float, slot_sums, precision=HIGHEST)
    group_max, group_sum = joined_all((group_max, group_sum), COL, combine_lse)
    return -(group_max + jnp.log(group_sum))


def col_potential_of(values, grouped, picker, live_float):
    slot_max = jnp.max(values, axis=1)
    group_max = jnp.max(jnp.where(grouped[:, :, None], slot_max[:, None, :], NEGATIVE), axis=0)
    shift_back = lookup_rows(picker, group_max)
    slot_sums = jnp.sum(jnp.exp(values - shift_back[:, None, :]), axis=1)
    group_sum = jnp.einsum("sr,sc->rc", live_float, slot_sums, precision=HIGHEST)
    group_max, group_sum = combined_all((group_max, group_sum), "row", combine_lse)
    return -(group_max + jnp.log(group_sum))


def on_device(features, adj_vals, blk_cols, blk_count, send_list, weight, cand_tiles, cand_count):
    feat_width = features.shape[2]
    outgoing = jax.vmap(pick_rows)(features, send_list[:, 0])
    ghost_rows = lax.all_to_all(outgoing, ROW_COL, split_axis=1, concat_axis=1, tiled=True)
    embedded = []
    for graph_id in range(2):
        lookup = jnp.concatenate([features[graph_id], ghost_rows[graph_id]], axis=0).reshape(
            -1, TILE, feat_width
        )
        embedded.append(
            aggregate(
                lookup,
                adj_vals[graph_id],
                blk_cols[graph_id],
                blk_count[graph_id],
                weight,
                features[graph_id],
            )
        )
    source_embed = embedded[0]
    target_embed = embedded[1]
    row_count = lax.axis_size("row")
    col_count = lax.axis_size(COL)
    rows_here = cand_tiles[0, 0, 0]
    cols_here = cand_tiles[0, 0, 1]
    slot_index = jnp.arange(CAP, dtype=jnp.int32)
    slot_live = slot_index < cand_count[0, 0]
    target_group = lax.all_gather(target_embed, "row", axis=0, tiled=True).reshape(
        -1, TILE, feat_width
    )
    target_tiles = target_group[cols_here]
    source_group = lax.all_gather(source_embed, COL, axis=0, tiled=True).reshape(
        -1, TILE, feat_width
    )
    source_tiles = source_group[rows_here]
    logits = (
        SHARPNESS
        / math.sqrt(feat_width)
        * jnp.einsum("sid,sjd->sij", source_tiles, target_tiles, precision=HIGHEST)
    )
    row_onehot = rows_here[:, None] == jnp.arange(TD * col_count, dtype=jnp.int32)[None, :]
    col_onehot = cols_here[:, None] == jnp.arange(TD * row_count, dtype=jnp.int32)[None, :]
    row_grouped = row_onehot & slot_live[:, None]
    col_grouped = col_onehot & slot_live[:, None]
    row_picker = row_onehot.astype(jnp.float32)
    col_picker = col_onehot.astype(jnp.float32)
    row_livef = row_grouped.astype(jnp.float32)
    col_livef = col_grouped.astype(jnp.float32)
    live_cube = slot_live[:, None, None]
    col_pot = jnp.zeros((TD * row_count, TILE), jnp.float32)
    row_pot = jnp.zeros((TD * col_count, TILE), jnp.float32)
    for sweep_id in range(ITERS):
        col_slot = lookup_rows(col_picker, col_pot)
        values = jnp.where(live_cube, logits + col_slot[:, None, :], NEGATIVE)
        row_pot = row_potential_of(values, row_grouped, row_picker, row_livef)
        row_slot = lookup_rows(row_picker, row_pot)
        values = jnp.where(live_cube, logits + row_slot[:, :, None], NEGATIVE)
        col_pot = col_potential_of(values, col_grouped, col_picker, col_livef)
    row_slot = lookup_rows(row_picker, row_pot)
    col_slot = lookup_rows(col_picker, col_pot)
    log_plan = jnp.where(live_cube, logits + row_slot[:, :, None] + col_slot[:, None, :], 0.0)
    return (
        log_plan[None, None],
        row_pot.reshape(1, col_count, -1),
        col_pot.reshape(row_count, 1, -1),
    )


def solution(mesh):
    finer = Mesh(
        mesh.devices.reshape(mesh.shape["row"], 2, 4, 2), ("row", "col_0", "col_1", "col_2")
    )
    placed = (
        P(None, ROW_COL, None),
        P(None, ROW_COL, None, None, None),
        P(None, ROW_COL, None),
        P(None, ROW_COL),
        P(None, ROW_COL, None),
        P(),
        P("row", COL, None, None),
        P("row", COL),
    )
    return jax.shard_map(
        on_device,
        mesh=finer,
        in_specs=placed,
        out_specs=(P("row", COL, None, None, None), P("row", None, None), P(None, COL, None)),
        check_vma=False,
    )
```

profile of v0, /device:TPU:1, one launch (start us, length us, event | category | flops | bytes accessed | tf_op | source)
XLA Modules:
  0.0 697.5 jit_solution(7761243411783571190)
XLA Ops:
  7.9 12.6 %gather_fusion.4 = f32[1024,256]{1,0:T(8,128)S(1)} fusion(f32[2,1024,256]{2,1,0:T(8,128)} %param.12, s32[1024]{0:T(1024)S(1)} %bitcast.240), kind=kCustom, calls=%fused_computation.4 | custom fusion | bytes 2105344 | tf_op jit(solution)/shard_map/vmap()/gather | solution.py:105
  22.4 11.5 %all-to-all-start = ((f32[2,512,256]{2,0,1:T(2,128)}), f32[2,512,256]{2,0,1:T(2,128)S(1)}, u32[]{:S(2)}, u32[]{:S(2)}) async-start(f32[2,512,256]{2,0,1:T(2,128)} %copy.24), calls=%async_computation | async-start | bytes 2097152 | tf_op jit(solution)/shard_map/all_to_all | solution.py:143
  34.0 12.8 %fusion.125 = (bf16[1,8,20,128,128]{4,3,2,1,0:T(8,128)(2,1)}, bf16[1,8,20,128,128]{4,3,2,1,0:T(8,128)(2,1)}) fusion(bf16[2,8,20,128,128]{4,3,2,1,0:T(8,128)(2,1)} %param.13), kind=kLoop, calls=%fused_computation.219 | loop fusion | bytes 20971520 | tf_op jit(solution)/shard_map/slice | solution.py:152
  48.5 12.7 %copy_bitcast_fusion = (bf16[8,20,128,128]{3,2,0,1:T(8,128)(2,1)}, bf16[8,20,128,128]{3,2,0,1:T(8,128)(2,1)}) fusion(bf16[1,8,20,128,128]{4,3,2,1,0:T(8,128)(2,1)} %get-tuple-element.195, bf16[1,8,20,128,128]{4,3,2,1,0:T(8,128)(2,1)} %get-tuple-element.196), kind=kLoop, calls=%fused_computation.33 | loop fusion | bytes 20971520 | tf_op jit(solution)/shard_map/squeeze | solution.py:152
  64.3 180.3 %while.27 = (s32[]{:T(128)}, f32[8,128,256]{2,1,0:T(8,128)}, f32[8,128]{1,0:T(8,128)S(1)}, s32[20]{0:T(128)S(1)}, bf16[8,20,128,128]{3,2,0,1:T(8,128)(2,1)}, /*i...) while((s32[]{:T(128)}, f32[8,128,256]{2,1,0:T(8,128)}, ...), condition=%wide.region_5.6_spmd.clone, body=%wide.region_3.5_spmd.clone.sunk | while | flops 403834912 | bytes 5788086 | solution.py:97
  250.6 186.6 %while.26 = (s32[]{:T(128)}, f32[8,128,256]{2,1,0:T(8,128)}, f32[8,128]{1,0:T(8,128)S(1)}, s32[20]{0:T(128)S(1)}, bf16[8,20,128,128]{3,2,0,1:T(8,128)(2,1)}, /*i...) while((s32[]{:T(128)}, f32[8,128,256]{2,1,0:T(8,128)}, ...), condition=%wide.region_2.3_spmd.clone, body=%wide.region_0.2_spmd.clone.sunk | while | flops 403834912 | bytes 5788086 | solution.py:97
  292.3 3.7 convolution_add_fusion.4
  441.8 7.0 %gather_fusion.3 = f32[48,128,256]{2,1,0:T(8,128)} fusion(f32[64,128,256]{2,1,0:T(8,128)} %bitcast.243, s32[1024]{0:T(1024)S(1)} %get-tuple-element.225), kind=kCustom, calls=%fused_computation.3 | custom fusion | bytes 12583104 | tf_op jit(solution)/shard_map/gather | solution.py:170
  448.9 85.5 %all-gather.7.cloned.1.call-done = f32[16384,256]{1,0:T(8,128)} async-done(((f32[1024,256]{1,0:T(8,128)}), f32[16384,256]{1,0:T(8,128)}) %all-gather.7.cloned.1.call-update) | async-done | bytes 16777232 | tf_op jit(solution)/shard_map/all_gather | solution.py:171
  534.4 9.4 %gather_fusion.2 = f32[48,128,256]{2,1,0:T(8,128)} fusion(f32[128,128,256]{2,1,0:T(8,128)} %bitcast.247, s32[1024]{0:T(1024)S(1)} %get-tuple-element.226), kind=kCustom, calls=%fused_computation.2 | custom fusion | bytes 12583104 | tf_op jit(solution)/shard_map/gather | solution.py:174
  543.7 9.2 %fusion.14 = (f32[48,128]{1,0:T(8,128)S(1)}, f32[48,128,128]{2,1,0:T(8,128)S(1)}) fusion(f32[48,128]{1,0:T(8,128)S(1)} %fusion.88, pred[48]{0:T(512)(128)(4,1)S(1)} %iota_compare_fusion.13, f32[48,128,256]{2,1,0:T(8,128)} %gather_fusion.2, f32[48,128,256]{2,1,0:T(8,128)} %gather_fusion.3), kind=kOutput, calls=%fused_computation.46 | convolution fusion | flops 2419058688 | bytes 15777840 | tf_op jit(solution)/shard_map/sid,sjd->sij/dot_general | solution.py:178
  554.4 3.8 all-gather
  560.6 3.8 all-gather.1
  564.5 9.4 %all_gather.66 = f32[4,128,128]{2,1,0:T(8,128)S(1)} all-gather(f32[1,128,128]{2,1,0:T(8,128)S(1)} %get-tuple-element.194), channel_id=1, replica_groups=mesh['row'=8,'col_0'=2,'col_1'=4,'col_2'=2] {'col_1'}, dimensions={0}, use_global_device_ids=true | all-gather | bytes 327680 | tf_op jit(solution)/shard_map/all_gather | solution.py:21
  573.8 10.2 %all_gather.70 = f32[4,128,128]{2,1,0:T(8,128)S(1)} all-gather(f32[1,128,128]{2,1,0:T(8,128)S(1)} %get-tuple-element.193), channel_id=1, replica_groups=mesh['row'=8,'col_0'=2,'col_1'=4,'col_2'=2] {'col_1'}, dimensions={0}, use_global_device_ids=true | all-gather | bytes 327680 | tf_op jit(solution)/shard_map/all_gather | solution.py:21
  584.2 9.4 %all_gather.67 = f32[2,128,128]{2,1,0:T(8,128)S(1)} all-gather(f32[1,128,128]{2,1,0:T(8,128)S(1)} %get-tuple-element.192), channel_id=1, replica_groups=mesh['row'=8,'col_0'=2,'col_1'=4,'col_2'=2] {'col_2'}, dimensions={0}, use_global_device_ids=true | all-gather | bytes 196608 | tf_op jit(solution)/shard_map/all_gather | solution.py:21
  599.2 17.5 %all_to_all.15 = f32[8,128,128]{2,1,0:T(8,128)S(1)} all-to-all(f32[8,128,128]{2,1,0:T(8,128)S(1)} %broadcast_in_dim.144), channel_id=1, replica_groups=mesh['row'=8,'col_0'=2,'col_1'=4,'col_2'=2] {'row'}, dimensions={0} | all-to-all | bytes 1048576 | tf_op jit(solution)/shard_map/all_to_all | solution.py:30
  619.7 3.8 all-gather.2
  626.0 3.8 all-gather.3
  629.8 9.4 %all_gather.74 = f32[4,128,128]{2,1,0:T(8,128)S(1)} all-gather(f32[1,128,128]{2,1,0:T(8,128)S(1)} %get-tuple-element.186), channel_id=1, replica_groups=mesh['row'=8,'col_0'=2,'col_1'=4,'col_2'=2] {'col_1'}, dimensions={0}, use_global_device_ids=true | all-gather | bytes 327680 | tf_op jit(solution)/shard_map/all_gather | solution.py:21
  639.2 9.4 %all_gather.78 = f32[4,128,128]{2,1,0:T(8,128)S(1)} all-gather(f32[1,128,128]{2,1,0:T(8,128)S(1)} %get-tuple-element.185), channel_id=1, replica_groups=mesh['row'=8,'col_0'=2,'col_1'=4,'col_2'=2] {'col_1'}, dimensions={0}, use_global_device_ids=true | all-gather | bytes 327680 | tf_op jit(solution)/shard_map/all_gather | solution.py:21
  649.2 10.8 %all_gather.75 = f32[2,128,128]{2,1,0:T(8,128)S(1)} all-gather(f32[1,128,128]{2,1,0:T(8,128)S(1)} %get-tuple-element.184), channel_id=1, replica_groups=mesh['row'=8,'col_0'=2,'col_1'=4,'col_2'=2] {'col_2'}, dimensions={0}, use_global_device_ids=true | all-gather | bytes 196608 | tf_op jit(solution)/shard_map/all_gather | solution.py:21
  670.3 4.2 all-to-all-start.2
  678.4 7.9 %all-to-all-done.2 = f32[8,128,128]{2,1,0:T(8,128)} async-done(((f32[8,128,128]{2,1,0:T(8,128)}), f32[8,128,128]{2,1,0:T(8,128)}, u32[]{:S(2)}, u32[]{:S(2)}) %all-to-all-start.2) | async-done | bytes 524320 | tf_op jit(solution)/shard_map/all_to_all | solution.py:30
  (428 shorter events, 338.7 us)
Async XLA Ops:
  7.2 238.9 %copy-start = (f32[256,256]{1,0:T(8,128)S(1)}, f32[256,256]{1,0:T(8,128)}, u32[]{:S(2)}) copy-start(f32[256,256]{1,0:T(8,128)} %param.17) | copy-start | bytes 786436
  22.4 38.9 %all-to-all-start = ((f32[2,512,256]{2,0,1:T(2,128)}), f32[2,512,256]{2,0,1:T(2,128)S(1)}, u32[]{:S(2)}, u32[]{:S(2)}) async-start(f32[2,512,256]{2,0,1:T(2,128)} %copy.24), calls=%async_computation | async-start | bytes 2097152 | tf_op jit(solution)/shard_map/all_to_all | solution.py:143
  33.9 408.0 %all-gather.9.cloned.1.call-start = ((), (), s32[]{:S(2)}) async-start(), calls=%async_computation.4 | async-start | bytes 9437184 | tf_op jit(solution)/shard_map/all_gather | solution.py:167
  34.0 12.9 %copy-start.11 = (s32[2,8]{1,0:T(2,128)S(1)}, s32[2,8]{1,0:T(2,128)}, u32[]{:S(2)}) copy-start(s32[2,8]{1,0:T(2,128)} %param.15) | copy-start | bytes 196
  34.0 12.9 %copy-start.7 = (s32[2,8,20]{2,1,0:T(8,128)S(1)}, s32[2,8,20]{2,1,0:T(8,128)}, u32[]{:S(2)}) copy-start(s32[2,8,20]{2,1,0:T(8,128)} %param.14) | copy-start | bytes 3844
  34.0 13.0 %copy-start.1 = (f32[2,1024,256]{2,1,0:T(8,128)S(1)}, f32[2,1024,256]{2,1,0:T(8,128)}, u32[]{:S(2)}) copy-start(f32[2,1024,256]{2,1,0:T(8,128)} %param.12) | copy-start | bytes 6291460
  61.3 1.7 copy-start.3
  244.6 3.8 copy-start.2
  248.1 286.3 %all-gather.7.cloned.1.call-start = ((), (), s32[]{:S(2)}) async-start(), calls=%async_computation.3 | async-start | bytes 17825792 | tf_op jit(solution)/shard_map/all_gather | solution.py:171
  437.3 4.1 copy-start.8
  441.4 175.4 %copy-start.9 = (s32[48]{0:T(128)}, s32[48]{0:T(128)S(1)}, u32[]{:S(2)}) copy-start(s32[48]{0:T(128)S(1)} %get-tuple-element.211) | copy-start | bytes 580
  660.1 0.7 copy-start.4
  665.2 4.0 copy-start.5
  665.2 4.0 copy-start.10
  670.3 16.0 %all-to-all-start.2 = ((f32[8,128,128]{2,1,0:T(8,128)}), f32[8,128,128]{2,1,0:T(8,128)}, u32[]{:S(2)}, u32[]{:S(2)}) async-start(f32[8,128,128]{2,1,0:T(8,128)} %broadcast_in_dim.147), calls=%async_computation.2 | async-start | bytes 1048576 | tf_op jit(solution)/shard_map/all_to_all | solution.py:30
  687.5 3.2 copy-start.6
Sparse Core Ops, SparseCore 0:
  248.2 110.0 all-gather.8
  440.8 93.4 all-gather.6
where the time goes:
time: 703 us; the launch traced here: 697 us
  local copies, waits for them, and re-layouts  171 us (24%)
  matrix products  154 us (22%)
  blocking collectives  95.2 us (14%)
  waiting for transfers between devices  93.4 us (13%)
  other arithmetic  77 us (11%)
  loops' own time  75.8 us (11%)
  starting transfers between devices  15.9 us (2%)
  between operations  15.3 us (2%)
    dot_general x40, matrix products, add_block(): jnp.einsum('tij,tjd->tid', weights_now, picked, precision=HIGHEST)  136 us
    all_gather x1, waiting for transfers between devices, on_device(): lax.all_gather(source_embed, COL, axis=0, tiled=True)  85.5 us
    gather x40, local copies, waits for them, and re-layouts, add_block(): picked = lookup[block_cols[:, block_index]]  81 us
    all_gather x12, blocking collectives, joined_all(): pieces = jax.tree.map(lambda part: lax.all_gather(part, axis), array)  77.7 us
    another operation x2, loops' own time, aggregate(): lax.scan(add_block, (start_sum, start_deg), jnp.arange(block_vals.shape[1]))  75.8 us
    reduce_sum x40, other arithmetic, add_block(): degree = degree + jnp.sum(weights_now, axis=2)  48.9 us
    dynamic_slice x40, local copies, waits for them, and re-layouts, aggregate(): lax.scan(add_block, (start_sum, start_deg), jnp.arange(block_vals.shape[1]))  23.6 us
    all_to_all x1, blocking collectives, from_everyone(): lax.all_to_all(jnp.broadcast_to(array[None], (size, *array.shape)), axis,...  17.5 us
  transfers between devices with their start and end apart: 4, of which 2 were waited for; matrix products, arithmetic and copies ran while one was open for 27% of the time, Pallas kernels for 0%

commit v1 on v0

--- a/solution.py
+++ b/solution.py
@@ -14,6 +14,16 @@
 HIGHEST = lax.Precision.HIGHEST
 SHARPNESS = 2.0
 NEGATIVE = -1e30
+
+
+def _direct_tiles(axis_tag, local_values, at_axis):
+    seen_now = jnp.concatenate(
+        lax.all_to_all(
+            jnp.stack([local_values for _ in range(lax.axis_size(axis_tag))], 0), axis_tag, 0, 0
+        ),
+        at_axis,
+    )
+    return seen_now
 
 
 def joined_all(array, axes, combine):
@@ -168,9 +178,7 @@
         -1, TILE, feat_width
     )
     target_tiles = target_group[cols_here]
-    source_group = lax.all_gather(source_embed, COL, axis=0, tiled=True).reshape(
-        -1, TILE, feat_width
-    )
+    source_group = _direct_tiles(COL, source_embed, 0).reshape(-1, TILE, feat_width)
     source_tiles = source_group[rows_here]
     logits = (
         SHARPNESS

time: 703 us -> 734 us (1.044)
  waiting for transfers between devices: 93.4 us -> 117 us
  local copies, waits for them, and re-layouts: 171 us -> 179 us
    all_gather x1, waiting for transfers between devices: 0.02 us -> 109 us  [on_device(): lax.all_gather(target_embed, 'row', axis=0, tiled=True)]
    all_gather x1 -> x0, waiting for transfers between devices: 85.5 us -> none  [on_device(): lax.all_gather(source_embed, COL, axis=0, tiled=True)]
  transfers between devices with their start and end apart: 4 -> 4, of which waited for: 2 -> 2; matrix products, arithmetic and copies ran while one was open for 27% -> 26% of each run, Pallas kernels for 0% -> 0%
where the time goes in v1:
time: 734 us; the launch traced here: 728 us
  local copies, waits for them, and re-layouts  179 us (24%)
  matrix products  151 us (21%)
  waiting for transfers between devices  117 us (16%)
  blocking collectives  92.2 us (13%)
  other arithmetic  76.8 us (10%)
  loops' own time  75.8 us (10%)
  starting transfers between devices  22.1 us (3%)
  between operations  15.2 us (2%)
    dot_general x40, matrix products, add_block(): jnp.einsum('tij,tjd->tid', weights_now, picked, precision=HIGHEST)  134 us
    all_gather x1, waiting for transfers between devices, on_device(): lax.all_gather(target_embed, 'row', axis=0, tiled=True)  109 us
    gather x40, local copies, waits for them, and re-layouts, add_block(): picked = lookup[block_cols[:, block_index]]  80.9 us
    all_gather x12, blocking collectives, joined_all(): pieces = jax.tree.map(lambda part: lax.all_gather(part, axis), array)  78 us
    another operation x2, loops' own time, aggregate(): lax.scan(add_block, (start_sum, start_deg), jnp.arange(block_vals.shape[1]))  75.8 us
    reduce_sum x40, other arithmetic, add_block(): degree = degree + jnp.sum(weights_now, axis=2)  48.9 us
    dynamic_slice x40, local copies, waits for them, and re-layouts, aggregate(): lax.scan(add_block, (start_sum, start_deg), jnp.arange(block_vals.shape[1]))  23.5 us
  transfers between devices with their start and end apart: 4, of which 2 were waited for; matrix products, arithmetic and copies ran while one was open for 26% of the time, Pallas kernels for 0%

profile of v1, /device:TPU:1, one launch (start us, length us, event | category | flops | bytes accessed | tf_op | source)
XLA Modules:
  0.0 727.9 jit_solution(10188799398789061428)
XLA Ops:
  7.9 12.6 %gather_fusion.4 = f32[1024,256]{1,0:T(8,128)S(1)} fusion(f32[2,1024,256]{2,1,0:T(8,128)} %param.12, s32[1024]{0:T(1024)S(1)} %bitcast.240), kind=kCustom, calls=%fused_computation.4 | custom fusion | bytes 2105344 | tf_op jit(solution)/shard_map/vmap()/gather | solution.py:115
  22.4 11.5 %all-to-all-start = ((f32[2,512,256]{2,0,1:T(2,128)}), f32[2,512,256]{2,0,1:T(2,128)S(1)}, u32[]{:S(2)}, u32[]{:S(2)}) async-start(f32[2,512,256]{2,0,1:T(2,128)} %copy.24), calls=%async_computation | async-start | bytes 2097152 | tf_op jit(solution)/shard_map/all_to_all | solution.py:153
  33.9 12.9 %fusion.125 = (bf16[1,8,20,128,128]{4,3,2,1,0:T(8,128)(2,1)}, bf16[1,8,20,128,128]{4,3,2,1,0:T(8,128)(2,1)}) fusion(bf16[2,8,20,128,128]{4,3,2,1,0:T(8,128)(2,1)} %param.13), kind=kLoop, calls=%fused_computation.219 | loop fusion | bytes 20971520 | tf_op jit(solution)/shard_map/slice | solution.py:162
  48.6 12.8 %copy_bitcast_fusion = (bf16[8,20,128,128]{3,2,0,1:T(8,128)(2,1)}, bf16[8,20,128,128]{3,2,0,1:T(8,128)(2,1)}) fusion(bf16[1,8,20,128,128]{4,3,2,1,0:T(8,128)(2,1)} %get-tuple-element.195, bf16[1,8,20,128,128]{4,3,2,1,0:T(8,128)(2,1)} %get-tuple-element.196), kind=kLoop, calls=%fused_computation.33 | loop fusion | bytes 20971520 | tf_op jit(solution)/shard_map/squeeze | solution.py:162
  64.3 180.5 %while.26 = (s32[]{:T(128)}, f32[8,128,256]{2,1,0:T(8,128)}, f32[8,128]{1,0:T(8,128)S(1)}, s32[20]{0:T(128)S(1)}, bf16[8,20,128,128]{3,2,0,1:T(8,128)(2,1)}, /*i...) while((s32[]{:T(128)}, f32[8,128,256]{2,1,0:T(8,128)}, ...), condition=%wide.region_2.3_spmd.clone, body=%wide.region_0.2_spmd.clone.sunk | while | flops 403834912 | bytes 5788086 | solution.py:107
  247.3 7.3 %stack.2 = f32[16,1024,256]{2,1,0:T(8,128)} broadcast(f32[1024,256]{1,0:T(8,128)S(1)} %fusion.18), dimensions={1,2} | broadcast | bytes 17825792 | tf_op jit(solution)/shard_map/stack | solution.py:22
  254.7 6.2 all-to-all-start.1
  263.5 184.0 %while.27 = (s32[]{:T(128)}, f32[8,128,256]{2,1,0:T(8,128)}, f32[8,128]{1,0:T(8,128)S(1)}, s32[20]{0:T(128)S(1)}, bf16[8,20,128,128]{3,2,0,1:T(8,128)(2,1)}, /*i...) while((s32[]{:T(128)}, f32[8,128,256]{2,1,0:T(8,128)}, ...), condition=%wide.region_5.6_spmd.clone, body=%wide.region_3.5_spmd.clone.sunk | while | flops 403834912 | bytes 5788086 | solution.py:107
  452.0 108.7 %all-gather.6.cloned.1.call-done = f32[8192,256]{1,0:T(8,128)} async-done(((f32[1024,256]{1,0:T(8,128)}), f32[8192,256]{1,0:T(8,128)}) %all-gather.6.cloned.1.call-update) | async-done | bytes 8388624 | tf_op jit(solution)/shard_map/all_gather | solution.py:177
  560.8 7.0 gather_fusion.3
  567.8 9.4 %gather_fusion.2 = f32[48,128,256]{2,1,0:T(8,128)} fusion(f32[128,128,256]{2,1,0:T(8,128)} %bitcast.11, s32[1024]{0:T(1024)S(1)} %get-tuple-element.226), kind=kCustom, calls=%fused_computation.2 | custom fusion | bytes 12583104 | tf_op jit(solution)/shard_map/gather | solution.py:182
  577.2 9.2 %fusion.14 = (f32[48,128]{1,0:T(8,128)S(1)}, f32[48,128,128]{2,1,0:T(8,128)S(1)}) fusion(f32[48,128]{1,0:T(8,128)S(1)} %fusion.88, pred[48]{0:T(512)(128)(4,1)S(1)} %iota_compare_fusion.13, f32[48,128,256]{2,1,0:T(8,128)} %gather_fusion.2, f32[48,128,256]{2,1,0:T(8,128)} %gather_fusion.3), kind=kOutput, calls=%fused_computation.46 | convolution fusion | flops 2419058688 | bytes 15777840 | tf_op jit(solution)/shard_map/sid,sjd->sij/dot_general | solution.py:186
  587.8 3.8 all-gather
  594.1 3.8 all-gather.1
  597.9 9.7 %all_gather.62 = f32[4,128,128]{2,1,0:T(8,128)S(1)} all-gather(f32[1,128,128]{2,1,0:T(8,128)S(1)} %get-tuple-element.194), channel_id=1, replica_groups=mesh['row'=8,'col_0'=2,'col_1'=4,'col_2'=2] {'col_1'}, dimensions={0}, use_global_device_ids=true | all-gather | bytes 327680 | tf_op jit(solution)/shard_map/all_gather | solution.py:31
  607.6 9.4 %all_gather.66 = f32[4,128,128]{2,1,0:T(8,128)S(1)} all-gather(f32[1,128,128]{2,1,0:T(8,128)S(1)} %get-tuple-element.193), channel_id=1, replica_groups=mesh['row'=8,'col_0'=2,'col_1'=4,'col_2'=2] {'col_1'}, dimensions={0}, use_global_device_ids=true | all-gather | bytes 327680 | tf_op jit(solution)/shard_map/all_gather | solution.py:31
  617.0 10.7 %all_gather.63 = f32[2,128,128]{2,1,0:T(8,128)S(1)} all-gather(f32[1,128,128]{2,1,0:T(8,128)S(1)} %get-tuple-element.192), channel_id=1, replica_groups=mesh['row'=8,'col_0'=2,'col_1'=4,'col_2'=2] {'col_2'}, dimensions={0}, use_global_device_ids=true | all-gather | bytes 196608 | tf_op jit(solution)/shard_map/all_gather | solution.py:31
  633.4 14.2 %all_to_all.20 = f32[8,128,128]{2,1,0:T(8,128)S(1)} all-to-all(f32[8,128,128]{2,1,0:T(8,128)S(1)} %broadcast_in_dim.144), channel_id=1, replica_groups=mesh['row'=8,'col_0'=2,'col_1'=4,'col_2'=2] {'row'}, dimensions={0} | all-to-all | bytes 1048576 | tf_op jit(solution)/shard_map/all_to_all | solution.py:40
  650.6 3.8 all-gather.2
  660.7 9.4 %all_gather.70 = f32[4,128,128]{2,1,0:T(8,128)S(1)} all-gather(f32[1,128,128]{2,1,0:T(8,128)S(1)} %get-tuple-element.186), channel_id=1, replica_groups=mesh['row'=8,'col_0'=2,'col_1'=4,'col_2'=2] {'col_1'}, dimensions={0}, use_global_device_ids=true | all-gather | bytes 327680 | tf_op jit(solution)/shard_map/all_gather | solution.py:31
  670.1 9.4 %all_gather.74 = f32[4,128,128]{2,1,0:T(8,128)S(1)} all-gather(f32[1,128,128]{2,1,0:T(8,128)S(1)} %get-tuple-element.185), channel_id=1, replica_groups=mesh['row'=8,'col_0'=2,'col_1'=4,'col_2'=2] {'col_1'}, dimensions={0}, use_global_device_ids=true | all-gather | bytes 327680 | tf_op jit(solution)/shard_map/all_gather | solution.py:31
  680.1 10.4 %all_gather.71 = f32[2,128,128]{2,1,0:T(8,128)S(1)} all-gather(f32[1,128,128]{2,1,0:T(8,128)S(1)} %get-tuple-element.184), channel_id=1, replica_groups=mesh['row'=8,'col_0'=2,'col_1'=4,'col_2'=2] {'col_2'}, dimensions={0}, use_global_device_ids=true | all-gather | bytes 196608 | tf_op jit(solution)/shard_map/all_gather | solution.py:31
  700.8 4.1 all-to-all-start.3
  708.8 7.9 %all-to-all-done.3 = f32[8,128,128]{2,1,0:T(8,128)} async-done(((f32[8,128,128]{2,1,0:T(8,128)}), f32[8,128,128]{2,1,0:T(8,128)}, u32[]{:S(2)}, u32[]{:S(2)}) %all-to-all-start.3) | async-done | bytes 524320 | tf_op jit(solution)/shard_map/all_to_all | solution.py:40
  (428 shorter events, 342.7 us)
Async XLA Ops:
  7.2 239.1 %copy-start = (f32[256,256]{1,0:T(8,128)S(1)}, f32[256,256]{1,0:T(8,128)}, u32[]{:S(2)}) copy-start(f32[256,256]{1,0:T(8,128)} %param.17) | copy-start | bytes 786436
  22.4 39.0 %all-to-all-start = ((f32[2,512,256]{2,0,1:T(2,128)}), f32[2,512,256]{2,0,1:T(2,128)S(1)}, u32[]{:S(2)}, u32[]{:S(2)}) async-start(f32[2,512,256]{2,0,1:T(2,128)} %copy.24), calls=%async_computation | async-start | bytes 2097152 | tf_op jit(solution)/shard_map/all_to_all | solution.py:153
  33.9 13.0 %copy-start.11 = (s32[2,8]{1,0:T(2,128)S(1)}, s32[2,8]{1,0:T(2,128)}, u32[]{:S(2)}) copy-start(s32[2,8]{1,0:T(2,128)} %param.15) | copy-start | bytes 196
  33.9 13.0 %copy-start.7 = (s32[2,8,20]{2,1,0:T(8,128)S(1)}, s32[2,8,20]{2,1,0:T(8,128)}, u32[]{:S(2)}) copy-start(s32[2,8,20]{2,1,0:T(8,128)} %param.14) | copy-start | bytes 3844
  33.9 13.2 %copy-start.1 = (f32[2,1024,256]{2,1,0:T(8,128)S(1)}, f32[2,1024,256]{2,1,0:T(8,128)}, u32[]{:S(2)}) copy-start(f32[2,1024,256]{2,1,0:T(8,128)} %param.12) | copy-start | bytes 6291460
  61.4 1.7 copy-start.3
  254.7 6.5 copy-start.2
  254.7 313.1 %all-to-all-start.1 = ((f32[16,1024,256]{2,1,0:T(8,128)}), f32[16,1024,256]{2,1,0:T(8,128)}, u32[]{:S(2)}, u32[]{:S(2)}) async-start(f32[16,1024,256]{2,1,0:T(8,128)} %stack.2), calls=%async_computation.1 | async-start | bytes 33554432 | tf_op jit(solution)/shard_map/all_to_all | solution.py:21
  260.9 299.9 %all-gather.6.cloned.1.call-start = ((), (), s32[]{:S(2)}) async-start(), calls=%async_computation.4 | async-start | bytes 9437184 | tf_op jit(solution)/shard_map/all_gather | solution.py:177
  447.5 4.1 copy-start.8
  451.7 196.1 %copy-start.9 = (s32[48]{0:T(128)}, s32[48]{0:T(128)S(1)}, u32[]{:S(2)}) copy-start(s32[48]{0:T(128)S(1)} %get-tuple-element.211) | copy-start | bytes 580
  690.5 0.7 copy-start.4
  695.7 4.0 copy-start.5
  695.7 4.0 copy-start.10
  700.8 15.9 %all-to-all-start.3 = ((f32[8,128,128]{2,1,0:T(8,128)}), f32[8,128,128]{2,1,0:T(8,128)}, u32[]{:S(2)}, u32[]{:S(2)}) async-start(f32[8,128,128]{2,1,0:T(8,128)} %broadcast_in_dim.147), calls=%async_computation.3 | async-start | bytes 1048576 | tf_op jit(solution)/shard_map/all_to_all | solution.py:40
  717.9 3.2 copy-start.6
Sparse Core Ops, SparseCore 0:
  451.1 109.6 all-gather.5
